TPU v7x, 32 devices: a whole 2x2x4 slice. The times are simulated.
32 devices in a mesh: seq: 4 (over z), fsdp: 8 (over y, x, core).
Axes of the slice: x: 2, y: 2, z: 4, core: 2. Of those that a mesh axis runs over, the one named last changes fastest.
Arguments:
- layer_input: bfloat16 [16, 512, 768], P('fsdp', 'seq'), may hold values from -20 to 20
- cotangent: bfloat16 [16, 512, 768], P('fsdp', 'seq'), may hold values from -6 to 6
- lengths: int32 [16], P('fsdp'), may hold values from 64 to 512, as said below
- project_weight: float32 [768, 2304], P('fsdp'), may hold values from -0.0625 to 0.0625
- output_weight: float32 [768, 768], P('fsdp'), may hold values from -2.5 to 2.5
- up_weight: float32 [768, 3072], P('fsdp'), may hold values from -0.21875 to 0.21875
- down_weight: float32 [3072, 768], P('fsdp'), may hold values from -0.109375 to 0.109375
- norm_gains: float32 [2, 768], P(None, 'fsdp'), may hold values from 0.5 to 1.5
- biases: float32 [6, 768], P(None, 'fsdp'), may hold values from -3 to 3
- hidden_bias: float32 [3072], P('fsdp'), may hold values from -3 to 3
- first_project: float32 [768, 2304], P('fsdp'), may hold values from -28 to 28
- first_output: float32 [768, 768], P('fsdp'), may hold values from -28 to 28
- first_up: float32 [768, 3072], P('fsdp'), may hold values from -28 to 28
- first_down: float32 [3072, 768], P('fsdp'), may hold values from -28 to 28
- first_gains: float32 [2, 768], P(None, 'fsdp'), may hold values from -28 to 28
- first_biases: float32 [6, 768], P(None, 'fsdp'), may hold values from -28 to 28
- first_hidden: float32 [3072], P('fsdp'), may hold values from -28 to 28
- second_project: float32 [768, 2304], P('fsdp'), may hold values from 1.6384 to 16.384
- second_output: float32 [768, 768], P('fsdp'), may hold values from 1.6384 to 16.384
- second_up: float32 [768, 3072], P('fsdp'), may hold values from 1.6384 to 16.384
- second_down: float32 [3072, 768], P('fsdp'), may hold values from 1.6384 to 16.384
- second_gains: float32 [2, 768], P(None, 'fsdp'), may hold values from 1.6384 to 16.384
- second_biases: float32 [6, 768], P(None, 'fsdp'), may hold values from 1.6384 to 16.384
- second_hidden: float32 [3072], P('fsdp'), may hold values from 1.6384 to 16.384
Outputs:
- block_output: bfloat16 [16, 512, 768], P('fsdp', 'seq')
- input_gradient: bfloat16 [16, 512, 768], P('fsdp', 'seq')
- project_gradient: float32 [768, 2304], P('fsdp')
- output_gradient: float32 [768, 768], P('fsdp')
- up_gradient: float32 [768, 3072], P('fsdp')
- down_gradient: float32 [3072, 768], P('fsdp')
- gains_gradient: float32 [2, 768], P(None, 'fsdp')
- biases_gradient: float32 [6, 768], P(None, 'fsdp')
- hidden_gradient: float32 [3072], P('fsdp')
- project_new: float32 [768, 2304], P('fsdp')
- output_new: float32 [768, 768], P('fsdp')
- up_new: float32 [768, 3072], P('fsdp')
- down_new: float32 [3072, 768], P('fsdp')
- gains_new: float32 [2, 768], P(None, 'fsdp')
- biases_new: float32 [6, 768], P(None, 'fsdp')
- hidden_new: float32 [3072], P('fsdp')
- first_project_new: float32 [768, 2304], P('fsdp')
- first_output_new: float32 [768, 768], P('fsdp')
- first_up_new: float32 [768, 3072], P('fsdp')
- first_down_new: float32 [3072, 768], P('fsdp')
- first_gains_new: float32 [2, 768], P(None, 'fsdp')
- first_biases_new: float32 [6, 768], P(None, 'fsdp')
- first_hidden_new: float32 [3072], P('fsdp')
- second_project_new: float32 [768, 2304], P('fsdp')
- second_output_new: float32 [768, 768], P('fsdp')
- second_up_new: float32 [768, 3072], P('fsdp')
- second_down_new: float32 [3072, 768], P('fsdp')
- second_gains_new: float32 [2, 768], P(None, 'fsdp')
- second_biases_new: float32 [6, 768], P(None, 'fsdp')
- second_hidden_new: float32 [3072], P('fsdp')
Inputs may be any that keep to these rules, and one draw needn't show every extreme that they name: Positions at and after lengths[s] of sequence s are padding keys; some sequence has all 512 positions real.
All inputs are finite; a program needn't handle non-finite values.
Results may differ from a plain program's by a relative error of at most 0.023.
The roundings to bfloat16 on the way count: a program that leaves them out, or rounds other values in their place, can miss the bound.
Values may be sent and summed in bfloat16 or wider, within the bound.
No kernel may reach another device: no remote copies, remote signals or barrier semaphores. Data moves between devices by JAX's collectives and lax.ppermute only.
A program may use at most 128 MiB of HBM per device.

v0:
```python
import jax
import jax.numpy as jnp
from jax import lax
from jax.sharding import PartitionSpec as P

HD = 64
ADAM_STEP = 3
beta_one = 0.9
beta_two = 0.999
learn_rate = 0.01
decay_rate = 0.01
adam_eps = 1e-08
norm_eps = 1e-05
half_root = 0.7071067811865476
gauss_peak = 0.3989422804014327


def layer_norm(summed, gain, shift):
    centred = summed - jnp.mean(summed, axis=-1, keepdims=True)
    spread = jnp.mean(centred * centred, axis=-1, keepdims=True)
    recip = lax.rsqrt(spread + norm_eps)
    normed = centred * recip
    return (normed * gain + shift, normed, recip)


def norm_back(upstream, normed, recip, gain):
    scaled = upstream * gain
    return recip * (
        scaled
        - jnp.mean(scaled, axis=-1, keepdims=True)
        - normed * jnp.mean(scaled * normed, axis=-1, keepdims=True)
    )


def gelu_exact(pre_act):
    return 0.5 * pre_act * (1.0 + lax.erf(pre_act * half_root))


def gelu_slope(pre_act):
    return (
        0.5 * (1.0 + lax.erf(pre_act * half_root))
        + pre_act * jnp.exp(-0.5 * pre_act * pre_act) * gauss_peak
    )


def contract_last(left, right):
    return lax.dot_general(
        left, right, (((1,), (1,)), ((), ())), preferred_element_type=jnp.float32
    )


def contract_first(left, right):
    return lax.dot_general(
        left, right, (((0,), (0,)), ((), ())), preferred_element_type=jnp.float32
    )


def split_heads(packed):
    token_count = packed.shape[0]
    return (
        packed[:, 0].reshape(token_count, -1, HD),
        packed[:, 1].reshape(token_count, -1, HD),
        packed[:, 2].reshape(token_count, -1, HD),
    )


def score_block(query_block, key_block, length):
    scores = jnp.einsum(
        "qhd,khd->hqk", query_block, key_block, preferred_element_type=jnp.float32
    ) * HD ** (-0.5)
    allowed = jnp.arange(key_block.shape[0])[None, None, :] < length
    return (scores, allowed)


def attend_forward(inputs):
    packed, length = inputs
    query_block, key_block, value_block = split_heads(packed)
    scores, allowed = score_block(query_block, key_block, length)
    masked = jnp.where(allowed, scores, -jnp.inf)
    row_max = jnp.max(masked, axis=-1, keepdims=True)
    lifted = jnp.exp(masked - row_max)
    row_total = jnp.sum(lifted, axis=-1, keepdims=True)
    weights16 = (lifted / row_total).astype(jnp.bfloat16)
    context = jnp.einsum("hqk,khd->qhd", weights16, value_block, preferred_element_type=jnp.float32)
    return (
        context.reshape(packed.shape[0], -1).astype(jnp.bfloat16),
        (row_max + jnp.log(row_total))[:, :, 0],
    )


def attend_backward(inputs):
    packed, context16, log_total, dcontext16, length = inputs
    query_block, key_block, value_block = split_heads(packed)
    token_count = packed.shape[0]
    scores, allowed = score_block(query_block, key_block, length)
    attention = jnp.where(allowed, jnp.exp(scores - log_total[:, :, None]), 0.0)
    weights16 = attention.astype(jnp.bfloat16)
    upstream = dcontext16.reshape(token_count, -1, HD)
    kept = context16.reshape(token_count, -1, HD)
    value_grad = jnp.einsum("hqk,qhd->khd", weights16, upstream, preferred_element_type=jnp.float32)
    prob_grad = jnp.einsum(
        "qhd,khd->hqk", upstream, value_block, preferred_element_type=jnp.float32
    )
    offset = jnp.sum(upstream.astype(jnp.float32) * kept.astype(jnp.float32), axis=-1)
    score_grad = attention * (prob_grad - jnp.transpose(offset)[:, :, None])
    score16 = (score_grad * HD ** (-0.5)).astype(jnp.bfloat16)
    query_grad = jnp.einsum("hqk,khd->qhd", score16, key_block, preferred_element_type=jnp.float32)
    key_grad = jnp.einsum("hqk,qhd->khd", score16, query_block, preferred_element_type=jnp.float32)
    stacked = jnp.stack(
        [
            query_grad.reshape(token_count, -1),
            key_grad.reshape(token_count, -1),
            value_grad.reshape(token_count, -1),
        ],
        axis=1,
    )
    return stacked.astype(jnp.bfloat16)


def adam_step(master, first, second, gradient, with_decay):
    first_new = beta_one * first + (1.0 - beta_one) * gradient
    second_new = beta_two * second + (1.0 - beta_two) * gradient * gradient
    first_hat = first_new / (1.0 - beta_one**ADAM_STEP)
    second_hat = second_new / (1.0 - beta_two**ADAM_STEP)
    change = first_hat / (jnp.sqrt(second_hat) + adam_eps)
    if with_decay:
        change = change + decay_rate * master
    return (master - learn_rate * change, first_new, second_new)


def shards(
    layer_input,
    cotangent,
    lengths,
    project_weight,
    output_weight,
    up_weight,
    down_weight,
    norm_gains,
    biases,
    hidden_bias,
    first_project,
    first_output,
    first_up,
    first_down,
    first_gains,
    first_biases,
    first_hidden,
    second_project,
    second_output,
    second_up,
    second_down,
    second_gains,
    second_biases,
    second_hidden,
):
    masters = (
        project_weight,
        output_weight,
        up_weight,
        down_weight,
        norm_gains,
        biases,
        hidden_bias,
    )
    firsts = (
        first_project,
        first_output,
        first_up,
        first_down,
        first_gains,
        first_biases,
        first_hidden,
    )
    seconds = (
        second_project,
        second_output,
        second_up,
        second_down,
        second_gains,
        second_biases,
        second_hidden,
    )
    rounded = [master.astype(jnp.bfloat16) for master in masters]
    gathered = (
        lax.all_gather(rounded[0], "fsdp", axis=0, tiled=True),
        lax.all_gather(rounded[1], "fsdp", axis=0, tiled=True),
        lax.all_gather(rounded[2], "fsdp", axis=0, tiled=True),
        lax.all_gather(rounded[3], "fsdp", axis=0, tiled=True),
        lax.all_gather(rounded[4], "fsdp", axis=1, tiled=True),
        lax.all_gather(rounded[5], "fsdp", axis=1, tiled=True),
        lax.all_gather(rounded[6], "fsdp", axis=0, tiled=True),
    )
    project16, output16, up16, down16, gains16, biases16, hidden16 = gathered
    gain_rows = gains16.astype(jnp.float32)
    bias_rows = biases16.astype(jnp.float32)
    hidden_row = hidden16.astype(jnp.float32)
    seqs_here, slice_len, model_width = layer_input.shape
    row_count = seqs_here * slice_len
    tokens16 = layer_input.reshape(row_count, model_width)
    shift = jnp.concatenate([bias_rows[0], jnp.zeros_like(bias_rows[0]), bias_rows[1]])
    packed = (jnp.dot(tokens16, project16, preferred_element_type=jnp.float32) + shift).astype(
        jnp.bfloat16
    )
    grouped = lax.all_to_all(
        packed.reshape(seqs_here, slice_len, 3, model_width),
        "seq",
        split_axis=3,
        concat_axis=1,
        tiled=True,
    )
    context_heads, log_total = lax.map(attend_forward, (grouped, lengths))
    context16 = lax.all_to_all(
        context_heads, "seq", split_axis=1, concat_axis=2, tiled=True
    ).reshape(row_count, model_width)
    inner_sum = (
        tokens16.astype(jnp.float32)
        + jnp.dot(context16, output16, preferred_element_type=jnp.float32)
        + bias_rows[2]
    )
    after_attend, norm_one, recip_one = layer_norm(inner_sum, gain_rows[0], bias_rows[3])
    after_attend16 = after_attend.astype(jnp.bfloat16)
    pre_act = jnp.dot(after_attend16, up16, preferred_element_type=jnp.float32) + hidden_row
    activated16 = gelu_exact(pre_act).astype(jnp.bfloat16)
    outer_sum = (
        after_attend
        + jnp.dot(activated16, down16, preferred_element_type=jnp.float32)
        + bias_rows[4]
    )
    final, norm_two, recip_two = layer_norm(outer_sum, gain_rows[1], bias_rows[5])
    block_output = final.astype(jnp.bfloat16).reshape(seqs_here, slice_len, model_width)
    back_project, back_output, back_up, back_down = (project16, output16, up16, down16)
    upstream = cotangent.reshape(row_count, model_width).astype(jnp.float32)
    grad_outer = norm_back(upstream, norm_two, recip_two, gain_rows[1])
    grad_outer16 = grad_outer.astype(jnp.bfloat16)
    grad_pre = contract_last(grad_outer16, back_down) * gelu_slope(pre_act)
    grad_pre16 = grad_pre.astype(jnp.bfloat16)
    grad_middle = grad_outer + contract_last(grad_pre16, back_up)
    grad_inner = norm_back(grad_middle, norm_one, recip_one, gain_rows[0])
    grad_inner16 = grad_inner.astype(jnp.bfloat16)
    grad_context16 = contract_last(grad_inner16, back_output).astype(jnp.bfloat16)
    grad_heads = lax.all_to_all(
        grad_context16.reshape(seqs_here, slice_len, model_width),
        "seq",
        split_axis=2,
        concat_axis=1,
        tiled=True,
    )
    packed_heads = lax.map(
        attend_backward, (grouped, context_heads, log_total, grad_heads, lengths)
    )
    packed_grad = lax.all_to_all(
        packed_heads, "seq", split_axis=1, concat_axis=3, tiled=True
    ).reshape(row_count, 3 * model_width)
    input_gradient = (
        (grad_inner + contract_last(packed_grad, back_project))
        .astype(jnp.bfloat16)
        .reshape(seqs_here, slice_len, model_width)
    )
    project_term = contract_first(tokens16, packed_grad)
    output_term = contract_first(context16, grad_inner16)
    up_term = contract_first(after_attend16, grad_pre16)
    down_term = contract_first(activated16, grad_outer16)
    gains_term = jnp.stack(
        [jnp.sum(grad_middle * norm_one, axis=0), jnp.sum(upstream * norm_two, axis=0)]
    )
    biases_term = jnp.stack(
        [
            jnp.sum(packed_grad[:, :model_width].astype(jnp.float32), axis=0),
            jnp.sum(packed_grad[:, 2 * model_width :].astype(jnp.float32), axis=0),
            jnp.sum(grad_inner, axis=0),
            jnp.sum(grad_middle, axis=0),
            jnp.sum(grad_outer, axis=0),
            jnp.sum(upstream, axis=0),
        ]
    )
    hidden_term = jnp.sum(grad_pre, axis=0)
    owned = (
        lax.psum_scatter(
            project_term.astype(jnp.bfloat16), "fsdp", scatter_dimension=0, tiled=True
        ).astype(jnp.float32),
        lax.psum_scatter(
            output_term.astype(jnp.bfloat16), "fsdp", scatter_dimension=0, tiled=True
        ).astype(jnp.float32),
        lax.psum_scatter(
            up_term.astype(jnp.bfloat16), "fsdp", scatter_dimension=0, tiled=True
        ).astype(jnp.float32),
        lax.psum_scatter(
            down_term.astype(jnp.bfloat16), "fsdp", scatter_dimension=0, tiled=True
        ).astype(jnp.float32),
        lax.psum_scatter(
            gains_term.astype(jnp.bfloat16), "fsdp", scatter_dimension=1, tiled=True
        ).astype(jnp.float32),
        lax.psum_scatter(
            biases_term.astype(jnp.bfloat16), "fsdp", scatter_dimension=1, tiled=True
        ).astype(jnp.float32),
        lax.psum_scatter(
            hidden_term.astype(jnp.bfloat16), "fsdp", scatter_dimension=0, tiled=True
        ).astype(jnp.float32),
    )
    totals = (
        lax.psum(owned[0].astype(jnp.bfloat16), "seq").astype(jnp.float32),
        lax.psum(owned[1].astype(jnp.bfloat16), "seq").astype(jnp.float32),
        lax.psum(owned[2].astype(jnp.bfloat16), "seq").astype(jnp.float32),
        lax.psum(owned[3].astype(jnp.bfloat16), "seq").astype(jnp.float32),
        lax.psum(owned[4].astype(jnp.bfloat16), "seq").astype(jnp.float32),
        lax.psum(owned[5].astype(jnp.bfloat16), "seq").astype(jnp.float32),
        lax.psum(owned[6].astype(jnp.bfloat16), "seq").astype(jnp.float32),
    )
    decay_flags = (True, True, True, True, False, False, False)
    results = [
        adam_step(
            masters[number], firsts[number], seconds[number], totals[number], decay_flags[number]
        )
        for number in range(7)
    ]
    new_masters = tuple((outcome[0] for outcome in results))
    new_firsts = tuple((outcome[1] for outcome in results))
    new_seconds = tuple((outcome[2] for outcome in results))
    return (block_output, input_gradient) + tuple(totals) + new_masters + new_firsts + new_seconds


def solution(mesh):
    return jax.shard_map(
        shards,
        mesh=mesh,
        in_specs=(
            P("fsdp", "seq", None),
            P("fsdp", "seq", None),
            P("fsdp"),
            P("fsdp", None),
            P("fsdp", None),
            P("fsdp", None),
            P("fsdp", None),
            P(None, "fsdp"),
            P(None, "fsdp"),
            P("fsdp"),
            P("fsdp", None),
            P("fsdp", None),
            P("fsdp", None),
            P("fsdp", None),
            P(None, "fsdp"),
            P(None, "fsdp"),
            P("fsdp"),
            P("fsdp", None),
            P("fsdp", None),
            P("fsdp", None),
            P("fsdp", None),
            P(None, "fsdp"),
            P(None, "fsdp"),
            P("fsdp"),
        ),
        out_specs=(
            P("fsdp", "seq", None),
            P("fsdp", "seq", None),
            P("fsdp", None),
            P("fsdp", None),
            P("fsdp", None),
            P("fsdp", None),
            P(None, "fsdp"),
            P(None, "fsdp"),
            P("fsdp"),
            P("fsdp", None),
            P("fsdp", None),
            P("fsdp", None),
            P("fsdp", None),
            P(None, "fsdp"),
            P(None, "fsdp"),
            P("fsdp"),
            P("fsdp", None),
            P("fsdp", None),
            P("fsdp", None),
            P("fsdp", None),
            P(None, "fsdp"),
            P(None, "fsdp"),
            P("fsdp"),
            P("fsdp", None),
            P("fsdp", None),
            P("fsdp", None),
            P("fsdp", None),
            P(None, "fsdp"),
            P(None, "fsdp"),
            P("fsdp"),
        ),
        check_vma=False,
    )
```

profile of v0, /device:TPU:0, one launch (start us, length us, event | category | flops | bytes accessed | tf_op | source)
XLA Modules:
  0.0 544.1 jit_solution(18204499861561235530)
XLA Ops:
  7.3 2.1 convert_element_type.182
  12.1 10.4 %all-gather = bf16[8,96,6]{1,2,0:T(8,128)(2,1)S(1)} all-gather(bf16[1,96,6]{1,2,0:T(8,128)(2,1)S(1)} %convert_bitcast_fusion), channel_id=1, replica_groups=mesh['seq'=4,'fsdp'=8] {'fsdp'}, dimensions={0}, use_global_device_ids=true | all-gather | bytes 10368 | tf_op jit(solution)/shard_map/all_gather | solution.py:191
  23.2 23.9 %all-gather.8.cloned.1.call-done = bf16[768,2304]{1,0:T(8,128)(2,1)} async-done(((bf16[96,2304]{1,0:T(8,128)(2,1)}), bf16[768,2304]{1,0:T(8,128)(2,1)}) %all-gather.8.cloned.1.call-update) | async-done | bytes 3538960 | tf_op jit(solution)/shard_map/all_gather | solution.py:186
  47.1 3.1 fusion.17
  50.7 3.1 copy.146
  53.9 4.7 all-to-all-start
  58.6 8.7 %all-gather.1 = bf16[8,96,2]{1,2,0:T(2,128)(2,1)S(1)} all-gather(bf16[1,96,2]{1,2,0:T(2,128)(2,1)S(1)} %convert_bitcast_fusion.1), channel_id=1, replica_groups=mesh['seq'=4,'fsdp'=8] {'fsdp'}, dimensions={0}, use_global_device_ids=true | all-gather | bytes 3456 | tf_op jit(solution)/shard_map/all_gather | solution.py:190
  67.4 20.2 %all-to-all-done = bf16[2,128,3,768]{1,0,2,3:T(2,128)(2,1)S(1)} async-done(((bf16[2,128,3,768]{1,0,2,3:T(2,128)(2,1)}), bf16[2,128,3,768]{1,0,2,3:T(2,128)(2,1)S(1)}, u32[]{:S(2)}, u32[]{:S(2)}) %all-to-all-start) | async-done | bytes 1179680 | tf_op jit(solution)/shard_map/all_to_all | solution.py:205
  87.9 9.0 %while.22 = (s32[]{:T(128)}, bf16[2,512,192]{1,2,0:T(8,128)(2,1)S(1)}, f32[2,3,512]{2,1,0:T(4,128)S(1)}, bf16[2,512,3,192]{1,3,2,0:T(8,128)(2,1)S(1)}, s32[2]{0:T(128)}, /*index=5*/s32[]{:T(128)}) while((s32[]{:T(128)}, bf16[2,512,192]{1,2,0:T(8,128)(2,1)S(1)}, f32[2,3,512]{2,1,0:T(4,128)S(1)}, bf16[2,512,3,192]{1,3,2,0:T(8,128)(2,1)S(1)}, ...), condition=%wide.region_3.4_spmd, body=%wide.region_0.3_spmd.sunk | while | flops 210861056 | bytes 13033569 | solution.py:212
  88.0 1.2 dynamic_slice.37
  92.5 1.2 dynamic_slice.37
  98.6 3.5 all-to-all-start.1
  102.2 9.4 %all-gather.2 = bf16[8,1,384]{2,1,0:T(2,128)(2,1)S(1)} all-gather(bf16[1,1,384]{2,1,0:T(2,128)(2,1)S(1)} %reshape.259), channel_id=1, replica_groups=mesh['seq'=4,'fsdp'=8] {'fsdp'}, dimensions={0}, use_global_device_ids=true | all-gather | bytes 6912 | tf_op jit(solution)/shard_map/all_gather | solution.py:192
  113.0 3.1 all-to-all-done.1
  116.7 1.9 fusion.64
  118.9 6.0 %multiply_convert_fusion.1 = (bf16[256,3072]{1,0:T(8,128)(2,1)}, f32[256,3072]{1,0:T(8,128)}) fusion(f32[3072]{0:T(1024)} %bitcast.243, bf16[768,3072]{1,0:T(8,128)(2,1)} %all-gather.12.cloned.1.call-done, f32[256,768]{1,0:T(8,128)S(1)} %get-tuple-element.339, f32[768]{0:T(1024)S(1)} %get-tuple-element.258, f32[768]{0:T(1024)S(1)} %get-tuple-element.263, ...), kind=kOutput, calls=%fused_computation.44 | convolution fusion | flops 1213661184 | bytes 10244096 | tf_op jit(solution)/shard_map/dot_general | solution.py:223
  124.9 31.0 %all-gather.14.cloned.1.call-done = bf16[3072,768]{1,0:T(8,128)(2,1)} async-done(((bf16[384,768]{1,0:T(8,128)(2,1)}), bf16[3072,768]{1,0:T(8,128)(2,1)}) %all-gather.14.cloned.1.call-update) | async-done | bytes 4718608 | tf_op jit(solution)/shard_map/all_gather | solution.py:189
  155.9 4.4 fusion.65
  161.6 1.7 fusion.59
  163.3 3.0 fusion.66
  166.3 2.2 multiply_reduce_fusion
  168.5 1.5 fusion.61
  170.1 1.5 convolution_convert_fusion.5
  171.7 5.2 convolution_convert_fusion.3
  176.9 1.8 convolution_convert_fusion.6
  179.8 4.6 all-to-all-start.2
  184.4 4.8 convolution_convert_fusion.2
  189.5 7.0 %all-to-all-done.2 = bf16[2,128,768]{1,0,2:T(2,128)(2,1)S(1)} async-done(((bf16[2,128,768]{1,0,2:T(2,128)(2,1)}), bf16[2,128,768]{1,0,2:T(2,128)(2,1)S(1)}, u32[]{:S(2)}, u32[]{:S(2)}) %all-to-all-start.2) | async-done | bytes 393248 | tf_op jit(solution)/shard_map/all_to_all | solution.py:242
  196.6 14.9 %while.23 = (s32[]{:T(128)}, bf16[2,512,3,192]{1,3,2,0:T(8,128)(2,1)}, bf16[2,512,3,192]{1,3,2,0:T(8,128)(2,1)S(1)}, s32[2]{0:T(128)}, f32[2,3,512]{2,1,0:T(4,12...) while((s32[]{:T(128)}, bf16[2,512,3,192]{1,3,2,0:T(8,128)(2,1)}, ...), condition=%wide.region_14.15_spmd, body=%wide.region_12.14_spmd.sunk | while | flops 514423808 | bytes 30316204 | solution.py:249
  197.5 1.2 dynamic_slice.41
  199.4 1.3 multiply_convert_fusion.3
  206.9 1.3 multiply_convert_fusion.3
  211.5 3.9 copy.155
  215.4 39.0 %all_to_all.66 = bf16[2,512,3,192]{3,0,2,1:T(2,128)(2,1)S(1)} all-to-all(bf16[2,512,3,192]{3,0,2,1:T(2,128)(2,1)S(1)} %copy.155), channel_id=1, replica_groups=mesh['seq'=4,'fsdp'=8] {'seq'}, dimensions={1} | all-to-all | bytes 2359296 | tf_op jit(solution)/shard_map/all_to_all | solution.py:252
  254.4 4.3 copy.156
  258.7 2.4 fusion.16
  261.1 4.0 copy.161
  268.8 54.0 %reduce-scatter.17.cloned.1.call-done = bf16[384,768]{1,0:T(8,128)(2,1)} async-done(((bf16[3072,768]{1,0:T(8,128)(2,1)}), bf16[384,768]{1,0:T(8,128)(2,1)}) %reduce-scatter.17.cloned.1.call-update) | async-done | bytes 589840 | tf_op jit(solution)/shard_map/reduce_scatter | solution.py:288
  322.8 51.4 %reduce-scatter.19.cloned.1.call-done = bf16[96,2304]{1,0:T(8,128)(2,1)} async-done(((bf16[768,2304]{1,0:T(8,128)(2,1)}), bf16[96,2304]{1,0:T(8,128)(2,1)}) %reduce-scatter.19.cloned.1.call-update) | async-done | bytes 442384 | tf_op jit(solution)/shard_map/reduce_scatter | solution.py:279
  375.6 12.8 %all-reduce = bf16[3072]{0:T(1024)(128)(2,1)S(1)} all-reduce(bf16[3072]{0:T(1024)(128)(2,1)S(1)} %copy-done.40), channel_id=8, replica_groups=mesh['seq'=4,'fsdp'=8] {'fsdp'}, use_global_device_ids=true, to_apply=%region_36.37.clone | all-reduce | flops 3072 | bytes 12288
  388.5 23.1 %reduce-scatter.21.cloned.1.call-done = bf16[96,2]{1,0:T(8,128)(2,1)} async-done(((bf16[768,2]{1,0:T(8,128)(2,1)}), bf16[96,2]{1,0:T(8,128)(2,1)}) %reduce-scatter.21.cloned.1.call-update) | async-done | bytes 400
  412.5 4.0 fusion.24
  416.5 32.2 %reduce-scatter.23.cloned.1.call-done = bf16[96,6]{1,0:T(8,128)(2,1)} async-done(((bf16[768,6]{1,0:T(8,128)(2,1)}), bf16[96,6]{1,0:T(8,128)(2,1)}) %reduce-scatter.23.cloned.1.call-update) | async-done | bytes 1168
  449.5 11.8 %all-reduce.1 = (bf16[2,96]{1,0:T(2,128)(2,1)S(1)}, bf16[6,96]{1,0:T(8,128)(2,1)S(1)}, bf16[384]{0:T(512)(128)(2,1)S(1)}) all-reduce(bf16[2,96]{1,0:T(2,128)(2,1)S(1)} %copy.164, bf16[6,96]{1,0:T(8,128)(2,1)S(1)} %copy.166, bf16[384]{0:T(512)(128)(2,1)S(1)} %dynamic-slice.1), channel_id=1, replica_groups=mesh['seq'=4,'fsdp'=8] {'seq'}, use_global_device_ids=true, to_apply=%region_26.27 | all-reduce | flops 1152 | bytes 4608 | tf_op jit(solution)/shard_map/psum | solution.py:306
  463.2 63.8 %all-reduce.5.cloned.1.call-done = (bf16[96,2304]{1,0:T(8,128)(2,1)}, bf16[96,768]{1,0:T(8,128)(2,1)}, bf16[96,3072]{1,0:T(8,128)(2,1)}, bf16[384,768]{1,0:T(8,128)(2,1)}) async-done(((bf16[96,2304]{1,0:T(8,128)(2,1)}, bf16[96,768]{1,0:T(8,128)(2,1)}, bf16[96,3072]{1,0:T(8,128)(2,1)}, bf16[384,768]{1,0:T(8,128)(2,1)}), (bf16[96,2304]{1,0:T(8,128)(2,1)}, bf16[96,768]{1,0:T(8,128)(2,1)}, ...) | async-done | bytes 1769488 | tf_op jit(solution)/shard_map/psum | solution.py:302
  527.0 4.4 multiply_subtract_fusion
  531.4 2.6 multiply_subtract_fusion.1
  534.5 2.0 multiply_subtract_fusion.2
  (247 shorter events, 37.7 us)
Async XLA Ops:
  7.2 3.0 copy-start.7
  7.2 39.9 %all-gather.8.cloned.1.call-start = ((), (), s32[]{:S(2)}) async-start(), calls=%async_computation.10 | async-start | bytes 3981312 | tf_op jit(solution)/shard_map/all_gather | solution.py:186
  9.4 107.3 %all-gather.10.cloned.1.call-start = ((), (), s32[]{:S(2)}) async-start(), calls=%async_computation.11 | async-start | bytes 1327104 | tf_op jit(solution)/shard_map/all_gather | solution.py:187
  10.2 108.7 %all-gather.12.cloned.1.call-start = ((), (), s32[]{:S(2)}) async-start(), calls=%async_computation.12 | async-start | bytes 5308416 | tf_op jit(solution)/shard_map/all_gather | solution.py:188
  11.1 36.0 %copy-start.23 = (bf16[2,128,768]{2,1,0:T(8,128)(2,1)S(1)}, bf16[2,128,768]{2,1,0:T(8,128)(2,1)}, u32[]{:S(2)}) copy-start(bf16[2,128,768]{2,1,0:T(8,128)(2,1)} %param.28) | copy-start | bytes 1179652
  11.1 144.8 %all-gather.14.cloned.1.call-start = ((), (), s32[]{:S(2)}) async-start(), calls=%async_computation.13 | async-start | bytes 5308416 | tf_op jit(solution)/shard_map/all_gather | solution.py:189
  53.9 4.7 copy-start.49
  53.9 33.7 %all-to-all-start = ((bf16[2,128,3,768]{1,0,2,3:T(2,128)(2,1)}), bf16[2,128,3,768]{1,0,2,3:T(2,128)(2,1)S(1)}, u32[]{:S(2)}, u32[]{:S(2)}) async-start(bf16[2,128,3,768]{1,0,2,3:T(2,128)(2,1)} %copy.146), calls=%async_computation | async-start | bytes 2359296 | tf_op jit(solution)/shard_map/all_to_all | solution.py:205
  97.5 4.7 copy-start.36
  97.5 14.8 %copy-start.3 = (bf16[2,128,768]{2,1,0:T(8,128)(2,1)S(1)}, bf16[2,128,768]{2,1,0:T(8,128)(2,1)}, u32[]{:S(2)}) copy-start(bf16[2,128,768]{2,1,0:T(8,128)(2,1)} %param.29) | copy-start | bytes 1179652
  97.5 19.2 %copy-start.24 = (bf16[2,128,768]{2,1,0:T(8,128)(2,1)S(1)}, bf16[2,128,768]{2,1,0:T(8,128)(2,1)}, u32[]{:S(2)}) copy-start(bf16[2,128,768]{2,1,0:T(8,128)(2,1)} %param.28) | copy-start | bytes 1179652
  98.6 17.5 %all-to-all-start.1 = ((bf16[2,512,192]{2,0,1:T(2,128)(2,1)}), bf16[2,512,192]{2,0,1:T(2,128)(2,1)S(1)}, u32[]{:S(2)}, u32[]{:S(2)}) async-start(bf16[2,512,192]{2,0,1:T(2,128)(2,1)} %copy.149), calls=%async_computation.1 | async-start | bytes 1048576 | tf_op jit(solution)/shard_map/all_to_all | solution.py:213
  102.1 166.7 %reduce-scatter.13.cloned.1.call-start = ((), (), s32[]{:S(2)}) async-start(), calls=%async_computation.14 | async-start | bytes 1327104 | tf_op jit(solution)/shard_map/reduce_scatter | solution.py:282
  118.8 47.4 %copy-start.33 = (f32[256]{0:T(256)}, f32[256]{0:T(256)S(1)}, u32[]{:S(2)}) copy-start(f32[256]{0:T(256)S(1)} %add_rsqrt_fusion.1) | copy-start | bytes 3076
  118.9 37.1 %copy-start.44 = (f32[768]{0:T(1024)S(1)}, f32[768]{0:T(1024)}, u32[]{:S(2)}) copy-start(f32[768]{0:T(1024)} %get-tuple-element.257) | copy-start | bytes 9220
  155.9 7.4 %copy-start.53 = (bf16[3072,768]{1,0:T(8,128)(2,1)S(1)}, bf16[3072,768]{1,0:T(8,128)(2,1)}, u32[]{:S(2)}) copy-start(bf16[3072,768]{1,0:T(8,128)(2,1)} %all-gather.14.cloned.1.call-done) | copy-start | bytes 14155780
  161.6 4.7 slice-start
  163.3 3.0 copy-start.11
  163.3 3.0 slice-start.1
  170.1 6.8 %copy-start.1 = (f32[256,768]{1,0:T(8,128)}, f32[256,768]{1,0:T(8,128)S(1)}, u32[]{:S(2)}) copy-start(f32[256,768]{1,0:T(8,128)S(1)} %get-tuple-element.326) | copy-start | bytes 2359300
  171.6 97.2 %reduce-scatter.15.cloned.1.call-start = ((), (), s32[]{:S(2)}) async-start(), calls=%async_computation.15 | async-start | bytes 5308416 | tf_op jit(solution)/shard_map/reduce_scatter | solution.py:285
  178.7 5.7 %copy-start.9 = (bf16[256,3072]{1,0:T(8,128)(2,1)S(1)}, bf16[256,3072]{1,0:T(8,128)(2,1)}, u32[]{:S(2)}) copy-start(bf16[256,3072]{1,0:T(8,128)(2,1)} %get-tuple-element.340) | copy-start | bytes 4718596
  179.8 16.7 %all-to-all-start.2 = ((bf16[2,128,768]{1,0,2:T(2,128)(2,1)}), bf16[2,128,768]{1,0,2:T(2,128)(2,1)S(1)}, u32[]{:S(2)}, u32[]{:S(2)}) async-start(bf16[2,128,768]{1,0,2:T(2,128)(2,1)} %copy.152), calls=%async_computation.2 | async-start | bytes 786432 | tf_op jit(solution)/shard_map/all_to_all | solution.py:242
  184.4 138.4 %reduce-scatter.17.cloned.1.call-start = ((), (), s32[]{:S(2)}) async-start(), calls=%async_computation.16 | async-start | bytes 5308416 | tf_op jit(solution)/shard_map/reduce_scatter | solution.py:288
  189.2 7.4 %copy-start.29 = (f32[2,3,512]{2,1,0:T(4,128)S(1)}, f32[2,3,512]{2,1,0:T(4,128)}, u32[]{:S(2)}) copy-start(f32[2,3,512]{2,1,0:T(4,128)} %copy-done.28) | copy-start | bytes 36868
  189.2 185.1 %reduce-scatter.19.cloned.1.call-start = ((), (), s32[]{:S(2)}) async-start(), calls=%async_computation.17 | async-start | bytes 3981312 | tf_op jit(solution)/shard_map/reduce_scatter | solution.py:279
  265.2 146.4 %reduce-scatter.21.cloned.1.call-start = ((), (), s32[]{:S(2)}) async-start(), calls=%async_computation.18 | async-start | bytes 221184
  267.3 181.5 %reduce-scatter.23.cloned.1.call-start = ((), (), s32[]{:S(2)}) async-start(), calls=%async_computation.19 | async-start | bytes 221184
  267.5 106.8 %copy-start.54 = (u32[32]{0:T(128)S(1)}, u32[32]{0:T(128)}, u32[]{:S(2)}) copy-start(u32[32]{0:T(128)} %constant.67) | copy-start | bytes 388
  267.5 108.1 %copy-start.40 = (bf16[3072]{0:T(1024)(128)(2,1)S(1)}, bf16[3072]{0:T(1024)(128)(2,1)}, u32[]{:S(2)}) copy-start(bf16[3072]{0:T(1024)(128)(2,1)} %get-tuple-element.345) | copy-start | bytes 18436
  267.5 144.9 %copy-start.2 = (f32[256,768]{1,0:T(8,128)S(1)}, f32[256,768]{1,0:T(8,128)}, u32[]{:S(2)}) copy-start(f32[256,768]{1,0:T(8,128)} %copy-done.1) | copy-start | bytes 2359300
  268.7 258.2 %all-reduce.5.cloned.1.call-start = ((), (), s32[]{:S(2)}) async-start(), calls=%async_computation.20 | async-start | bytes 3538944 | tf_op jit(solution)/shard_map/psum | solution.py:302
  412.4 48.9 %copy-start.50 = (f32[2,96]{1,0:T(2,128)S(1)}, f32[2,96]{1,0:T(2,128)}, u32[]{:S(2)}) copy-start(f32[2,96]{1,0:T(2,128)} %param.35) | copy-start | bytes 2308
  412.4 48.9 %copy-start.51 = (f32[2,96]{1,0:T(2,128)S(1)}, f32[2,96]{1,0:T(2,128)}, u32[]{:S(2)}) copy-start(f32[2,96]{1,0:T(2,128)} %param.42) | copy-start | bytes 2308
  412.4 48.9 %copy-start.52 = (f32[2,96]{1,0:T(2,128)S(1)}, f32[2,96]{1,0:T(2,128)}, u32[]{:S(2)}) copy-start(f32[2,96]{1,0:T(2,128)} %param.49) | copy-start | bytes 2308
  412.4 49.5 %copy-start.37 = (f32[384]{0:T(512)S(1)}, f32[384]{0:T(512)}, u32[]{:S(2)}) copy-start(f32[384]{0:T(512)} %param.37) | copy-start | bytes 4612
  412.5 49.5 %copy-start.45 = (f32[384]{0:T(512)S(1)}, f32[384]{0:T(512)}, u32[]{:S(2)}) copy-start(f32[384]{0:T(512)} %param.44) | copy-start | bytes 4612
  412.5 49.5 %copy-start.46 = (f32[384]{0:T(512)S(1)}, f32[384]{0:T(512)}, u32[]{:S(2)}) copy-start(f32[384]{0:T(512)} %param.51) | copy-start | bytes 4612
  412.5 50.1 %copy-start.32 = (f32[6,96]{1,0:T(8,128)S(1)}, f32[6,96]{1,0:T(8,128)}, u32[]{:S(2)}) copy-start(f32[6,96]{1,0:T(8,128)} %param.36) | copy-start | bytes 6916
  412.5 50.1 %copy-start.42 = (f32[6,96]{1,0:T(8,128)S(1)}, f32[6,96]{1,0:T(8,128)}, u32[]{:S(2)}) copy-start(f32[6,96]{1,0:T(8,128)} %param.43) | copy-start | bytes 6916
  412.5 50.0 %copy-start.43 = (f32[6,96]{1,0:T(8,128)S(1)}, f32[6,96]{1,0:T(8,128)}, u32[]{:S(2)}) copy-start(f32[6,96]{1,0:T(8,128)} %param.50) | copy-start | bytes 6916
  412.5 114.4 %copy-start.6 = (f32[384,768]{1,0:T(8,128)S(1)}, f32[384,768]{1,0:T(8,128)}, u32[]{:S(2)}) copy-start(f32[384,768]{1,0:T(8,128)} %param.34) | copy-start | bytes 3538948
  527.0 4.4 copy-start.8
  527.0 4.4 copy-start.13
  527.0 4.4 copy-start.14
  527.0 4.4 copy-start.21
  531.4 2.7 copy-start.20
  531.4 3.1 copy-start.22
  (26 other events, 41.1 us)
Sparse Core Ops, SparseCore 0:
  10.5 36.5 all-gather.7
  49.5 23.9 all-gather.9
  76.0 38.8 all-gather.11
  117.1 38.7 all-gather.13
  171.7 36.6 reduce-scatter.12
  211.8 53.7 reduce-scatter.14
  269.1 53.7 reduce-scatter.16
  326.3 47.9 reduce-scatter.18
  377.9 33.6 reduce-scatter.20
  415.0 33.6 reduce-scatter.22
  451.4 75.5 all-reduce.4
where the time goes:
time: 545 us; the launch traced here: 544 us
  waiting for transfers between devices  310 us (57%)
  blocking collectives  92.1 us (17%)
  matrix products  51 us (9%)
  local copies, waits for them, and re-layouts  35 us (6%)
  other arithmetic  27 us (5%)
  between operations  15.3 us (3%)
  starting transfers between devices  13.4 us (2%)
    psum x1, waiting for transfers between devices, shards(): lax.psum(owned[0].astype(jnp.bfloat16), 'seq').astype(jnp.float32)  63.8 us
    unnamed x13, waiting for transfers between devices  55.6 us
    reduce_scatter x1, waiting for transfers between devices, shards(): lax.psum_scatter(down_term.astype(jnp.bfloat16), 'fsdp', scatter_dimensio...  54 us
    reduce_scatter x1, waiting for transfers between devices, shards(): lax.psum_scatter(project_term.astype(jnp.bfloat16), 'fsdp', scatter_dimen...  51.4 us
    all_to_all x1, blocking collectives, shards(): lax.all_to_all(packed_heads, 'seq', split_axis=1, concat_axis=3, tiled=True)  39 us
    all_gather x1, waiting for transfers between devices, shards(): lax.all_gather(rounded[3], 'fsdp', axis=0, tiled=True)  31 us
    all_gather x1, waiting for transfers between devices, shards(): lax.all_gather(rounded[0], 'fsdp', axis=0, tiled=True)  23.9 us
    all_to_all x1, waiting for transfers between devices, shards(): lax.all_to_all(packed.reshape(seqs_here, slice_len, 3, model_width), 'seq...  20.2 us
  transfers between devices with their start and end apart: 14, of which 10 were waited for; matrix products, arithmetic and copies ran while one was open for 15% of the time, Pallas kernels for 0%

commit v1 on v0

--- a/solution.py
+++ b/solution.py
@@ -299,7 +299,7 @@
         ).astype(jnp.float32),
     )
     totals = (
-        lax.psum(owned[0].astype(jnp.bfloat16), "seq").astype(jnp.float32),
+        jnp.sum(lax.all_gather(owned[0].astype(jnp.bfloat16), "seq"), axis=0).astype(jnp.float32),
         lax.psum(owned[1].astype(jnp.bfloat16), "seq").astype(jnp.float32),
         lax.psum(owned[2].astype(jnp.bfloat16), "seq").astype(jnp.float32),
         lax.psum(owned[3].astype(jnp.bfloat16), "seq").astype(jnp.float32),

time: 545 us -> 565 us (1.037)
  waiting for transfers between devices: 310 us -> 362 us
  blocking collectives: 92.1 us -> 53.4 us
    all_to_all x1 -> x0, blocking collectives: 39 us -> none  [shards(): lax.all_to_all(packed_heads, 'seq', split_axis=1, concat_axis=3, tiled=True)]
    all_to_all x0 -> x1, waiting for transfers between devices: none -> 35.4 us  [shards(): lax.all_to_all(packed_heads, 'seq', split_axis=1, concat_axis=3, tiled=True)]
    all_gather x0 -> x1, waiting for transfers between devices: none -> 32.3 us  [shards(): lax.all_gather(owned[0].astype(jnp.bfloat16), 'seq')]
    psum x1, waiting for transfers between devices: 63.8 us -> 49.2 us  [shards(): lax.psum(owned[1].astype(jnp.bfloat16), 'seq').astype(jnp.float32)]
    unnamed x13 -> x14, waiting for transfers between devices: 55.6 us -> 56.2 us
  transfers between devices with their start and end apart: 14 -> 16, of which waited for: 10 -> 12; matrix products, arithmetic and copies ran while one was open for 15% -> 16% of each run, Pallas kernels for 0% -> 0%
where the time goes in v1:
time: 565 us; the launch traced here: 564 us
  waiting for transfers between devices  362 us (64%)
  blocking collectives  53.4 us (9%)
  matrix products  51 us (9%)
  local copies, waits for them, and re-layouts  35.8 us (6%)
  other arithmetic  29.3 us (5%)
  starting transfers between devices  17 us (3%)
  between operations  15.7 us (3%)
    unnamed x14, waiting for transfers between devices  56.2 us
    reduce_scatter x1, waiting for transfers between devices, shards(): lax.psum_scatter(down_term.astype(jnp.bfloat16), 'fsdp', scatter_dimensio...  52.5 us
    reduce_scatter x1, waiting for transfers between devices, shards(): lax.psum_scatter(project_term.astype(jnp.bfloat16), 'fsdp', scatter_dimen...  50.6 us
    psum x1, waiting for transfers between devices, shards(): lax.psum(owned[1].astype(jnp.bfloat16), 'seq').astype(jnp.float32)  49.2 us
    all_to_all x1, waiting for transfers between devices, shards(): lax.all_to_all(packed_heads, 'seq', split_axis=1, concat_axis=3, tiled=True)  35.4 us
    all_gather x1, waiting for transfers between devices, shards(): lax.all_gather(owned[0].astype(jnp.bfloat16), 'seq')  32.3 us
    all_gather x1, waiting for transfers between devices, shards(): lax.all_gather(rounded[3], 'fsdp', axis=0, tiled=True)  31 us
    all_gather x1, waiting for transfers between devices, shards(): lax.all_gather(rounded[0], 'fsdp', axis=0, tiled=True)  23.9 us
  transfers between devices with their start and end apart: 16, of which 12 were waited for; matrix products, arithmetic and copies ran while one was open for 16% of the time, Pallas kernels for 0%

profile of v1, /device:TPU:0, one launch (start us, length us, event | category | flops | bytes accessed | tf_op | source)
XLA Modules:
  0.0 564.2 jit_solution(13844290000231152977)
XLA Ops:
  7.3 2.1 convert_element_type.184
  12.1 10.4 %all-gather.1 = bf16[8,96,6]{1,2,0:T(8,128)(2,1)S(1)} all-gather(bf16[1,96,6]{1,2,0:T(8,128)(2,1)S(1)} %convert_bitcast_fusion), channel_id=1, replica_groups=mesh['seq'=4,'fsdp'=8] {'fsdp'}, dimensions={0}, use_global_device_ids=true | all-gather | bytes 10368 | tf_op jit(solution)/shard_map/all_gather | solution.py:191
  23.2 23.9 %all-gather.10.cloned.1.call-done = bf16[768,2304]{1,0:T(8,128)(2,1)} async-done(((bf16[96,2304]{1,0:T(8,128)(2,1)}), bf16[768,2304]{1,0:T(8,128)(2,1)}) %all-gather.10.cloned.1.call-update) | async-done | bytes 3538960 | tf_op jit(solution)/shard_map/all_gather | solution.py:186
  47.1 3.1 fusion.17
  50.7 3.1 copy.110
  53.9 4.7 all-to-all-start
  58.6 8.7 %all-gather.2 = bf16[8,96,2]{1,2,0:T(2,128)(2,1)S(1)} all-gather(bf16[1,96,2]{1,2,0:T(2,128)(2,1)S(1)} %convert_bitcast_fusion.1), channel_id=1, replica_groups=mesh['seq'=4,'fsdp'=8] {'fsdp'}, dimensions={0}, use_global_device_ids=true | all-gather | bytes 3456 | tf_op jit(solution)/shard_map/all_gather | solution.py:190
  67.4 20.2 %all-to-all-done = bf16[2,128,3,768]{1,0,2,3:T(2,128)(2,1)S(1)} async-done(((bf16[2,128,3,768]{1,0,2,3:T(2,128)(2,1)}), bf16[2,128,3,768]{1,0,2,3:T(2,128)(2,1)S(1)}, u32[]{:S(2)}, u32[]{:S(2)}) %all-to-all-start) | async-done | bytes 1179680 | tf_op jit(solution)/shard_map/all_to_all | solution.py:205
  87.9 9.0 %while.22 = (s32[]{:T(128)}, bf16[2,512,192]{1,2,0:T(8,128)(2,1)S(1)}, f32[2,3,512]{2,1,0:T(4,128)S(1)}, bf16[2,512,3,192]{1,3,2,0:T(8,128)(2,1)S(1)}, s32[2]{0:T(128)}, /*index=5*/s32[]{:T(128)}) while((s32[]{:T(128)}, bf16[2,512,192]{1,2,0:T(8,128)(2,1)S(1)}, f32[2,3,512]{2,1,0:T(4,128)S(1)}, bf16[2,512,3,192]{1,3,2,0:T(8,128)(2,1)S(1)}, ...), condition=%wide.region_3.4_spmd, body=%wide.region_0.3_spmd.sunk | while | flops 210861056 | bytes 13033569 | solution.py:212
  98.6 3.5 all-to-all-start.1
  102.2 9.4 %all-gather.3 = bf16[8,1,384]{2,1,0:T(2,128)(2,1)S(1)} all-gather(bf16[1,1,384]{2,1,0:T(2,128)(2,1)S(1)} %reshape.260), channel_id=1, replica_groups=mesh['seq'=4,'fsdp'=8] {'fsdp'}, dimensions={0}, use_global_device_ids=true | all-gather | bytes 6912 | tf_op jit(solution)/shard_map/all_gather | solution.py:192
  113.0 3.1 all-to-all-done.1
  116.7 1.9 fusion.64
  118.9 6.1 %multiply_convert_fusion.1 = (bf16[256,3072]{1,0:T(8,128)(2,1)}, f32[256,3072]{1,0:T(8,128)}) fusion(f32[3072]{0:T(1024)} %bitcast.245, bf16[768,3072]{1,0:T(8,128)(2,1)} %all-gather.14.cloned.1.call-done, f32[256,768]{1,0:T(8,128)S(1)} %get-tuple-element.188, f32[768]{0:T(1024)S(1)} %get-tuple-element.108, f32[768]{0:T(1024)S(1)} %get-tuple-element.113, ...), kind=kOutput, calls=%fused_computation.44 | convolution fusion | flops 1213661184 | bytes 10244096 | tf_op jit(solution)/shard_map/dot_general | solution.py:223
  125.0 31.0 %all-gather.16.cloned.1.call-done = bf16[3072,768]{1,0:T(8,128)(2,1)} async-done(((bf16[384,768]{1,0:T(8,128)(2,1)}), bf16[3072,768]{1,0:T(8,128)(2,1)}) %all-gather.16.cloned.1.call-update) | async-done | bytes 4718608 | tf_op jit(solution)/shard_map/all_gather | solution.py:189
  155.9 4.4 fusion.65
  161.6 1.7 fusion.59
  163.3 3.0 fusion.66
  166.3 2.2 multiply_reduce_fusion
  168.5 1.5 fusion.61
  170.1 1.5 convolution_convert_fusion.5
  171.7 5.1 convolution_convert_fusion.3
  176.8 1.8 convolution_convert_fusion.6
  179.7 4.6 all-to-all-start.2
  184.4 4.8 convolution_convert_fusion.2
  189.2 7.3 %all-to-all-done.2 = bf16[2,128,768]{1,0,2:T(2,128)(2,1)S(1)} async-done(((bf16[2,128,768]{1,0,2:T(2,128)(2,1)}), bf16[2,128,768]{1,0,2:T(2,128)(2,1)S(1)}, u32[]{:S(2)}, u32[]{:S(2)}) %all-to-all-start.2) | async-done | bytes 393248 | tf_op jit(solution)/shard_map/all_to_all | solution.py:242
  196.6 14.9 %while.23 = (s32[]{:T(128)}, bf16[2,512,3,192]{1,3,2,0:T(8,128)(2,1)}, bf16[2,512,3,192]{1,3,2,0:T(8,128)(2,1)S(1)}, s32[2]{0:T(128)}, f32[2,3,512]{2,1,0:T(4,12...) while((s32[]{:T(128)}, bf16[2,512,3,192]{1,3,2,0:T(8,128)(2,1)}, ...), condition=%wide.region_14.15_spmd, body=%wide.region_12.14_spmd.sunk | while | flops 514423808 | bytes 30316204 | solution.py:249
  206.8 1.3 multiply_convert_fusion.3
  211.5 4.9 copy.119
  216.4 3.7 all-to-all-start.3
  221.2 35.4 %all-to-all-done.3 = bf16[2,512,3,192]{3,0,2,1:T(2,128)(2,1)S(1)} async-done(((bf16[2,512,3,192]{3,0,2,1:T(2,128)(2,1)}), bf16[2,512,3,192]{3,0,2,1:T(2,128)(2,1)S(1)}, u32[]{:S(2)}, u32[]{:S(2)}) %all-to-all-start.3) | async-done | bytes 1179680 | tf_op jit(solution)/shard_map/all_to_all | solution.py:252
  256.6 4.3 copy.120
  260.9 2.4 fusion.16
  263.3 4.0 copy.125
  270.3 52.5 %reduce-scatter.17.cloned.1.call-done = bf16[384,768]{1,0:T(8,128)(2,1)} async-done(((bf16[3072,768]{1,0:T(8,128)(2,1)}), bf16[384,768]{1,0:T(8,128)(2,1)}) %reduce-scatter.17.cloned.1.call-update) | async-done | bytes 589840 | tf_op jit(solution)/shard_map/reduce_scatter | solution.py:288
  324.2 12.8 %all-reduce = bf16[3072]{0:T(1024)(128)(2,1)S(1)} all-reduce(bf16[3072]{0:T(1024)(128)(2,1)S(1)} %copy-done.38), channel_id=9, replica_groups=mesh['seq'=4,'fsdp'=8] {'fsdp'}, use_global_device_ids=true, to_apply=%region_36.37.clone | all-reduce | flops 3072 | bytes 12288
  337.1 23.1 %reduce-scatter.21.cloned.1.call-done = bf16[96,2]{1,0:T(8,128)(2,1)} async-done(((bf16[768,2]{1,0:T(8,128)(2,1)}), bf16[96,2]{1,0:T(8,128)(2,1)}) %reduce-scatter.21.cloned.1.call-update) | async-done | bytes 400
  361.0 50.6 %reduce-scatter.19.cloned.1.call-done = bf16[96,2304]{1,0:T(8,128)(2,1)} async-done(((bf16[768,2304]{1,0:T(8,128)(2,1)}), bf16[96,2304]{1,0:T(8,128)(2,1)}) %reduce-scatter.19.cloned.1.call-update) | async-done | bytes 442384 | tf_op jit(solution)/shard_map/reduce_scatter | solution.py:279
  411.8 4.0 fusion.24
  415.8 33.0 %reduce-scatter.23.cloned.1.call-done = bf16[96,6]{1,0:T(8,128)(2,1)} async-done(((bf16[768,6]{1,0:T(8,128)(2,1)}), bf16[96,6]{1,0:T(8,128)(2,1)}) %reduce-scatter.23.cloned.1.call-update) | async-done | bytes 1168
  449.5 12.0 %all-reduce.1 = (bf16[2,96]{1,0:T(2,128)(2,1)S(1)}, bf16[6,96]{1,0:T(8,128)(2,1)S(1)}, bf16[384]{0:T(512)(128)(2,1)S(1)}) all-reduce(bf16[2,96]{1,0:T(2,128)(2,1)S(1)} %copy.128, bf16[6,96]{1,0:T(8,128)(2,1)S(1)} %copy.130, bf16[384]{0:T(512)(128)(2,1)S(1)} %dynamic-slice.1), channel_id=1, replica_groups=mesh['seq'=4,'fsdp'=8] {'seq'}, use_global_device_ids=true, to_apply=%region_26.27 | all-reduce | flops 1152 | bytes 4608 | tf_op jit(solution)/shard_map/psum | solution.py:306
  463.4 49.2 %all-reduce.5.cloned.1.call-done = (bf16[96,768]{1,0:T(8,128)(2,1)}, bf16[96,3072]{1,0:T(8,128)(2,1)}, bf16[384,768]{1,0:T(8,128)(2,1)}) async-done(((bf16[96,768]{1,0:T(8,128)(2,1)}, bf16[96,3072]{1,0:T(8,128)(2,1)}, bf16[384,768]{1,0:T(8,128)(2,1)}), (bf16[96,768]{1,0:T(8,128)(2,1)}, bf16[96,3072]{1,0:T(8,128)(2,1)}, bf16[384,768]{1,0:T(8,128)(2,1)})) %all-reduce.5.cloned.1.call-update) | async-done | bytes 1327120 | tf_op jit(solution)/shard_map/psum | solution.py:303
  512.7 2.2 multiply_subtract_fusion.3
  514.9 3.9 multiply_subtract_fusion
  518.8 2.5 multiply_subtract_fusion.1
  521.4 32.3 %all-gather.18.cloned.1.call-done = bf16[384,2304]{1,0:T(8,128)(2,1)} async-done(((bf16[96,2304]{1,0:T(8,128)(2,1)}), bf16[384,2304]{1,0:T(8,128)(2,1)}) %all-gather.18.cloned.1.call-update) | async-done | bytes 1769488 | tf_op jit(solution)/shard_map/all_gather | solution.py:302
  553.6 1.8 reduce_sum.191
  555.4 2.0 multiply_subtract_fusion.2
  (248 shorter events, 41.2 us)
Async XLA Ops:
  7.2 39.9 %all-gather.10.cloned.1.call-start = ((), (), s32[]{:S(2)}) async-start(), calls=%async_computation.10 | async-start | bytes 3981312 | tf_op jit(solution)/shard_map/all_gather | solution.py:186
  9.4 107.3 %all-gather.12.cloned.1.call-start = ((), (), s32[]{:S(2)}) async-start(), calls=%async_computation.11 | async-start | bytes 1327104 | tf_op jit(solution)/shard_map/all_gather | solution.py:187
  10.2 108.7 %all-gather.14.cloned.1.call-start = ((), (), s32[]{:S(2)}) async-start(), calls=%async_computation.12 | async-start | bytes 5308416 | tf_op jit(solution)/shard_map/all_gather | solution.py:188
  11.1 36.0 %copy-start.24 = (bf16[2,128,768]{2,1,0:T(8,128)(2,1)S(1)}, bf16[2,128,768]{2,1,0:T(8,128)(2,1)}, u32[]{:S(2)}) copy-start(bf16[2,128,768]{2,1,0:T(8,128)(2,1)} %param.28) | copy-start | bytes 1179652
  11.1 144.8 %all-gather.16.cloned.1.call-start = ((), (), s32[]{:S(2)}) async-start(), calls=%async_computation.13 | async-start | bytes 5308416 | tf_op jit(solution)/shard_map/all_gather | solution.py:189
  53.9 4.7 copy-start.47
  53.9 33.7 %all-to-all-start = ((bf16[2,128,3,768]{1,0,2,3:T(2,128)(2,1)}), bf16[2,128,3,768]{1,0,2,3:T(2,128)(2,1)S(1)}, u32[]{:S(2)}, u32[]{:S(2)}) async-start(bf16[2,128,3,768]{1,0,2,3:T(2,128)(2,1)} %copy.110), calls=%async_computation | async-start | bytes 2359296 | tf_op jit(solution)/shard_map/all_to_all | solution.py:205
  97.5 4.7 copy-start.34
  97.5 14.8 %copy-start.3 = (bf16[2,128,768]{2,1,0:T(8,128)(2,1)S(1)}, bf16[2,128,768]{2,1,0:T(8,128)(2,1)}, u32[]{:S(2)}) copy-start(bf16[2,128,768]{2,1,0:T(8,128)(2,1)} %param.29) | copy-start | bytes 1179652
  97.5 19.2 %copy-start.25 = (bf16[2,128,768]{2,1,0:T(8,128)(2,1)S(1)}, bf16[2,128,768]{2,1,0:T(8,128)(2,1)}, u32[]{:S(2)}) copy-start(bf16[2,128,768]{2,1,0:T(8,128)(2,1)} %param.28) | copy-start | bytes 1179652
  98.6 17.5 %all-to-all-start.1 = ((bf16[2,512,192]{2,0,1:T(2,128)(2,1)}), bf16[2,512,192]{2,0,1:T(2,128)(2,1)S(1)}, u32[]{:S(2)}, u32[]{:S(2)}) async-start(bf16[2,512,192]{2,0,1:T(2,128)(2,1)} %copy.113), calls=%async_computation.1 | async-start | bytes 1048576 | tf_op jit(solution)/shard_map/all_to_all | solution.py:213
  102.1 168.2 %reduce-scatter.13.cloned.1.call-start = ((), (), s32[]{:S(2)}) async-start(), calls=%async_computation.14 | async-start | bytes 1327104 | tf_op jit(solution)/shard_map/reduce_scatter | solution.py:282
  118.8 47.4 %copy-start.31 = (f32[256]{0:T(256)}, f32[256]{0:T(256)S(1)}, u32[]{:S(2)}) copy-start(f32[256]{0:T(256)S(1)} %add_rsqrt_fusion.1) | copy-start | bytes 3076
  118.9 37.1 %copy-start.42 = (f32[768]{0:T(1024)S(1)}, f32[768]{0:T(1024)}, u32[]{:S(2)}) copy-start(f32[768]{0:T(1024)} %get-tuple-element.107) | copy-start | bytes 9220
  155.9 7.4 %copy-start.51 = (bf16[3072,768]{1,0:T(8,128)(2,1)S(1)}, bf16[3072,768]{1,0:T(8,128)(2,1)}, u32[]{:S(2)}) copy-start(bf16[3072,768]{1,0:T(8,128)(2,1)} %all-gather.16.cloned.1.call-done) | copy-start | bytes 14155780
  161.6 4.7 slice-start
  170.1 6.7 %copy-start.1 = (f32[256,768]{1,0:T(8,128)}, f32[256,768]{1,0:T(8,128)S(1)}, u32[]{:S(2)}) copy-start(f32[256,768]{1,0:T(8,128)S(1)} %get-tuple-element.175) | copy-start | bytes 2359300
  171.6 98.7 %reduce-scatter.15.cloned.1.call-start = ((), (), s32[]{:S(2)}) async-start(), calls=%async_computation.15 | async-start | bytes 5308416 | tf_op jit(solution)/shard_map/reduce_scatter | solution.py:285
  178.6 5.7 %copy-start.9 = (bf16[256,3072]{1,0:T(8,128)(2,1)S(1)}, bf16[256,3072]{1,0:T(8,128)(2,1)}, u32[]{:S(2)}) copy-start(bf16[256,3072]{1,0:T(8,128)(2,1)} %get-tuple-element.189) | copy-start | bytes 4718596
  179.7 16.7 %all-to-all-start.2 = ((bf16[2,128,768]{1,0,2:T(2,128)(2,1)}), bf16[2,128,768]{1,0,2:T(2,128)(2,1)S(1)}, u32[]{:S(2)}, u32[]{:S(2)}) async-start(bf16[2,128,768]{1,0,2:T(2,128)(2,1)} %copy.116), calls=%async_computation.2 | async-start | bytes 786432 | tf_op jit(solution)/shard_map/all_to_all | solution.py:242
  184.4 138.5 %reduce-scatter.17.cloned.1.call-start = ((), (), s32[]{:S(2)}) async-start(), calls=%async_computation.16 | async-start | bytes 5308416 | tf_op jit(solution)/shard_map/reduce_scatter | solution.py:288
  189.1 7.4 %copy-start.27 = (f32[2,3,512]{2,1,0:T(4,128)S(1)}, f32[2,3,512]{2,1,0:T(4,128)}, u32[]{:S(2)}) copy-start(f32[2,3,512]{2,1,0:T(4,128)} %copy-done.26) | copy-start | bytes 36868
  216.4 40.2 %all-to-all-start.3 = ((bf16[2,512,3,192]{3,0,2,1:T(2,128)(2,1)}), bf16[2,512,3,192]{3,0,2,1:T(2,128)(2,1)S(1)}, u32[]{:S(2)}, u32[]{:S(2)}) async-start(bf16[2,512,3,192]{3,0,2,1:T(2,128)(2,1)} %copy.119), calls=%async_computation.3 | async-start | bytes 3145728 | tf_op jit(solution)/shard_map/all_to_all | solution.py:252
  220.1 140.0 %reduce-scatter.21.cloned.1.call-start = ((), (), s32[]{:S(2)}) async-start(), calls=%async_computation.19 | async-start | bytes 221184
  221.1 190.5 %reduce-scatter.19.cloned.1.call-start = ((), (), s32[]{:S(2)}) async-start(), calls=%async_computation.18 | async-start | bytes 3981312 | tf_op jit(solution)/shard_map/reduce_scatter | solution.py:279
  267.4 181.3 %reduce-scatter.23.cloned.1.call-start = ((), (), s32[]{:S(2)}) async-start(), calls=%async_computation.20 | async-start | bytes 221184
  269.0 53.9 %copy-start.52 = (u32[32]{0:T(128)S(1)}, u32[32]{0:T(128)}, u32[]{:S(2)}) copy-start(u32[32]{0:T(128)} %constant.68) | copy-start | bytes 388
  269.0 55.2 %copy-start.38 = (bf16[3072]{0:T(1024)(128)(2,1)S(1)}, bf16[3072]{0:T(1024)(128)(2,1)}, u32[]{:S(2)}) copy-start(bf16[3072]{0:T(1024)(128)(2,1)} %get-tuple-element.194) | copy-start | bytes 18436
  269.0 142.6 %copy-start.2 = (f32[256,768]{1,0:T(8,128)S(1)}, f32[256,768]{1,0:T(8,128)}, u32[]{:S(2)}) copy-start(f32[256,768]{1,0:T(8,128)} %copy-done.1) | copy-start | bytes 2359300
  270.2 242.4 %all-reduce.5.cloned.1.call-start = ((), (), s32[]{:S(2)}) async-start(), calls=%async_computation.21 | async-start | bytes 2654208 | tf_op jit(solution)/shard_map/psum | solution.py:303
  322.9 230.8 %all-gather.18.cloned.1.call-start = ((), (), s32[]{:S(2)}) async-start(), calls=%async_computation.17 | async-start | bytes 2211840 | tf_op jit(solution)/shard_map/all_gather | solution.py:302
  411.6 50.0 %copy-start.48 = (f32[2,96]{1,0:T(2,128)S(1)}, f32[2,96]{1,0:T(2,128)}, u32[]{:S(2)}) copy-start(f32[2,96]{1,0:T(2,128)} %param.35) | copy-start | bytes 2308
  411.6 49.9 %copy-start.49 = (f32[2,96]{1,0:T(2,128)S(1)}, f32[2,96]{1,0:T(2,128)}, u32[]{:S(2)}) copy-start(f32[2,96]{1,0:T(2,128)} %param.42) | copy-start | bytes 2308
  411.7 49.9 %copy-start.50 = (f32[2,96]{1,0:T(2,128)S(1)}, f32[2,96]{1,0:T(2,128)}, u32[]{:S(2)}) copy-start(f32[2,96]{1,0:T(2,128)} %param.49) | copy-start | bytes 2308
  411.7 50.5 %copy-start.35 = (f32[384]{0:T(512)S(1)}, f32[384]{0:T(512)}, u32[]{:S(2)}) copy-start(f32[384]{0:T(512)} %param.37) | copy-start | bytes 4612
  411.7 50.5 %copy-start.43 = (f32[384]{0:T(512)S(1)}, f32[384]{0:T(512)}, u32[]{:S(2)}) copy-start(f32[384]{0:T(512)} %param.44) | copy-start | bytes 4612
  411.7 50.5 %copy-start.44 = (f32[384]{0:T(512)S(1)}, f32[384]{0:T(512)}, u32[]{:S(2)}) copy-start(f32[384]{0:T(512)} %param.51) | copy-start | bytes 4612
  411.7 51.1 %copy-start.30 = (f32[6,96]{1,0:T(8,128)S(1)}, f32[6,96]{1,0:T(8,128)}, u32[]{:S(2)}) copy-start(f32[6,96]{1,0:T(8,128)} %param.36) | copy-start | bytes 6916
  411.7 51.1 %copy-start.40 = (f32[6,96]{1,0:T(8,128)S(1)}, f32[6,96]{1,0:T(8,128)}, u32[]{:S(2)}) copy-start(f32[6,96]{1,0:T(8,128)} %param.43) | copy-start | bytes 6916
  411.7 51.1 %copy-start.41 = (f32[6,96]{1,0:T(8,128)S(1)}, f32[6,96]{1,0:T(8,128)}, u32[]{:S(2)}) copy-start(f32[6,96]{1,0:T(8,128)} %param.50) | copy-start | bytes 6916
  411.7 100.9 %copy-start.17 = (f32[96,768]{1,0:T(8,128)S(1)}, f32[96,768]{1,0:T(8,128)}, u32[]{:S(2)}) copy-start(f32[96,768]{1,0:T(8,128)} %param.32) | copy-start | bytes 884740
  411.8 103.1 %copy-start.13 = (f32[384,768]{1,0:T(8,128)S(1)}, f32[384,768]{1,0:T(8,128)}, u32[]{:S(2)}) copy-start(f32[384,768]{1,0:T(8,128)} %param.41) | copy-start | bytes 3538948
  415.8 99.1 %copy-start.6 = (f32[384,768]{1,0:T(8,128)S(1)}, f32[384,768]{1,0:T(8,128)}, u32[]{:S(2)}) copy-start(f32[384,768]{1,0:T(8,128)} %param.34) | copy-start | bytes 3538948
  514.9 3.9 copy-start.8
  514.9 3.9 copy-start.14
  518.8 36.6 %copy-start.21 = (f32[96,2304]{1,0:T(8,128)S(1)}, f32[96,2304]{1,0:T(8,128)}, u32[]{:S(2)}) copy-start(f32[96,2304]{1,0:T(8,128)} %param.45) | copy-start | bytes 2654212
  521.3 34.1 %copy-start.10 = (f32[96,2304]{1,0:T(8,128)S(1)}, f32[96,2304]{1,0:T(8,128)}, u32[]{:S(2)}) copy-start(f32[96,2304]{1,0:T(8,128)} %param.31) | copy-start | bytes 2654212
  521.3 34.1 %copy-start.20 = (f32[96,2304]{1,0:T(8,128)S(1)}, f32[96,2304]{1,0:T(8,128)}, u32[]{:S(2)}) copy-start(f32[96,2304]{1,0:T(8,128)} %param.38) | copy-start | bytes 2654212
  (26 other events, 51.5 us)
Sparse Core Ops, SparseCore 0:
  10.5 36.5 all-gather.9
  49.5 23.9 all-gather.11
  76.0 38.8 all-gather.13
  117.1 38.7 all-gather.15
  171.7 36.6 reduce-scatter.12
  211.8 53.7 reduce-scatter.14
  269.0 53.7 reduce-scatter.16
  326.4 33.6 reduce-scatter.20
  363.6 47.9 reduce-scatter.18
  415.0 33.6 reduce-scatter.22
  451.3 61.2 all-reduce.4
  514.1 39.4 all-gather.17
